TPU v7x, 512 devices: a whole 4x8x8 slice. The times are simulated.
512 devices in a mesh: seq: 128 (over z, y, core), tp: 4 (over x).
Axes of the slice: x: 4, y: 8, z: 8, core: 2. Of those that a mesh axis runs over, the one named last changes fastest.
Arguments:
- queries: bfloat16 [32768, 4096], P('seq', 'tp'), may hold values from -6 to 6, as said below
- keys: bfloat16 [32768, 512], P('seq', 'tp'), may hold values from -6 to 6, as said below
- values: bfloat16 [32768, 512], P('seq', 'tp'), may hold values from -6 to 6
- segment: int32 [32768], P('seq'), may hold values from 0 to 255, never falling along the last dimension, each value on 1 to 512 neighbouring positions
- repack: int32 [32768], P('seq'), may hold values from 0 to 32767, as said below
- proj: bfloat16 [1536, 4096], P('seq', 'tp'), may hold values from -0.5 to 0.5
- student_states: bfloat16 [32768, 1536], P('seq'), may hold values from -6 to 6
- target_row: int32 [32768], P('seq'), may hold values from 0 to 255
Outputs:
- student_rows: bfloat16 [32768, 1536], P('seq', 'tp')
- grad: float32 [1536, 4096], P('seq', 'tp')
Inputs may be any that keep to these rules, and one draw needn't show every extreme that they name: `queries`: scaled normal entries. `keys`: scaled normal entries. `repack`: A permutation of the student rows. Each device's teacher rows go in consecutive groups of 4 rows, in order, each group to one student owner (the device holding student rows owner * 256 to owner * 256 + 255); every device sends exactly 4 rows to each of 64 other devices and none to itself, so at most 4 rows from one device to one owner, reached by every sending pair.
All inputs are finite; a program needn't handle non-finite values.
Results may differ from a plain program's by a relative error of at most 0.0056.
Values may be sent and summed in bfloat16 or wider, within the bound.
No kernel may reach another device: no remote copies, remote signals or barrier semaphores. Data moves between devices by JAX's collectives and lax.ppermute only.
A program may use at most 64 MiB of HBM per device.

v0:
```python
import math
import jax
import jax.numpy as jnp
from jax import lax
from jax.sharding import PartitionSpec as P

HEADS = 32
KV_HEADS = 4
HEAD_DIM = 128
SW = 1536
REACH = 2
GROUP_ROWS = 4
neg_large = -1e30


def passed_along(block, axis, distance):
    devices = range(lax.axis_size(axis))
    route = [(i - distance, i) for i in devices if i - distance in devices]
    return lax.ppermute(block, axis, route)


def attend(queries, keys, values, segment):
    row_count = queries.shape[0]
    lanes = keys.shape[1]
    seg_rows = (segment + 1).astype(jnp.bfloat16).reshape(-1, lanes)
    seg_rows = jnp.concatenate([seg_rows, jnp.zeros((14, lanes), jnp.bfloat16)], 0)
    packed = jnp.concatenate([keys, values, seg_rows], 0)
    blocks = [packed]
    for step in range(1, REACH + 1):
        blocks.insert(0, passed_along(packed, "seq", step))
    all_keys = jnp.concatenate([b[:row_count] for b in blocks], 0)
    all_values = jnp.concatenate([b[row_count : 2 * row_count] for b in blocks], 0)
    key_seg = jnp.concatenate(
        [b[2 * row_count : 2 * row_count + 2].reshape(-1) for b in blocks], 0
    ).astype(jnp.int32)
    key_pos = jnp.arange(3 * row_count, dtype=jnp.int32) - REACH * row_count
    row_pos = jnp.arange(row_count, dtype=jnp.int32)
    allowed = (key_seg[None, :] == (segment + 1)[:, None]) & (key_pos[None, :] <= row_pos[:, None])
    group = HEADS // KV_HEADS
    q_heads = queries.reshape(row_count, group, HEAD_DIM)
    scale = 1.0 / math.sqrt(HEAD_DIM)
    outputs = []
    for head in range(group):
        scores = (
            jnp.einsum("td,sd->ts", q_heads[:, head], all_keys, preferred_element_type=jnp.float32)
            * scale
        )
        scores = jnp.where(allowed, scores, neg_large)
        top = jnp.max(scores, axis=-1, keepdims=True)
        expo = jnp.exp(scores - top)
        weights = (expo / jnp.sum(expo, axis=-1, keepdims=True)).astype(jnp.bfloat16)
        mixed = jnp.einsum("ts,sd->td", weights, all_values, preferred_element_type=jnp.float32)
        outputs.append(mixed.astype(jnp.bfloat16))
    return jnp.concatenate(outputs, axis=1)


def on_device(queries, keys, values, segment, repack, proj, student_states, target_row):
    row_count = queries.shape[0]
    devices = lax.axis_size("seq")
    groups = row_count // GROUP_ROWS
    attended = attend(queries, keys, values, segment)
    target_dev = repack // row_count
    local_slot = repack - target_dev * row_count
    owners = target_dev.reshape(groups, GROUP_ROWS)[:, 0]
    owner_hot = owners[None, :] == jnp.arange(devices, dtype=jnp.int32)[:, None]
    slots_by_group = local_slot.reshape(groups, GROUP_ROWS)
    slot_table = jnp.sum(jnp.where(owner_hot[:, :, None], slots_by_group[None], 0), axis=1)
    slot_table = jnp.where(jnp.any(owner_hot, axis=1)[:, None], slot_table, row_count)
    slots = lax.all_to_all(slot_table, "seq", split_axis=0, concat_axis=0, tiled=True)
    width_share = SW // lax.axis_size("tp")
    tp_index = lax.axis_index("tp")
    targets = student_states[target_row]
    bucket_dev = jnp.arange(devices * GROUP_ROWS, dtype=jnp.int32) // GROUP_ROWS
    bucket_pos = jnp.arange(devices * GROUP_ROWS, dtype=jnp.int32) % GROUP_ROWS
    row_ids = jnp.arange(row_count, dtype=jnp.int32)
    pick = (
        (bucket_dev[:, None] == target_dev[None, :])
        & (bucket_pos[:, None] == (row_ids % GROUP_ROWS)[None, :])
    ).astype(jnp.bfloat16)
    buckets = jnp.dot(pick, attended, preferred_element_type=jnp.float32).astype(jnp.bfloat16)
    arrived = lax.all_to_all(buckets, "seq", split_axis=0, concat_axis=0, tiled=True)
    place = (row_ids[:, None] == slots.reshape(-1)[None, :]).astype(jnp.bfloat16)
    student_x = jnp.dot(place, arrived, preferred_element_type=jnp.float32).astype(jnp.bfloat16)
    all_proj = lax.all_gather(proj, "seq", axis=0, tiled=True)
    y_part = jnp.einsum("tf,nf->tn", student_x, all_proj, preferred_element_type=jnp.float32)
    y_total = lax.psum(y_part, "tp")
    y_rounded = y_total.astype(jnp.bfloat16)
    delta = (y_rounded.astype(jnp.float32) - targets.astype(jnp.float32)).astype(jnp.bfloat16)
    out_rows = lax.dynamic_slice_in_dim(y_rounded, tp_index * width_share, width_share, 1)
    norm_factor = 1.0 / math.sqrt(row_count * devices)
    grad_rows = delta.shape[1] // devices
    term = jnp.einsum("ts,tf->sf", delta, student_x, preferred_element_type=jnp.float32)
    pieces = term.reshape(devices, grad_rows, term.shape[1])
    summed = lax.all_to_all(
        pieces.astype(jnp.bfloat16), "seq", split_axis=0, concat_axis=0, tiled=True
    ).astype(pieces.dtype)
    grad = jnp.sum(summed, axis=0) * norm_factor
    return (out_rows, grad)


def solution(mesh):
    placed = (
        P("seq", "tp"),
        P("seq", "tp"),
        P("seq", "tp"),
        P("seq"),
        P("seq"),
        P("seq", "tp"),
        P("seq", None),
        P("seq"),
    )
    return jax.shard_map(
        on_device,
        mesh=mesh,
        in_specs=placed,
        out_specs=(P("seq", "tp"), P("seq", "tp")),
        check_vma=False,
    )
```

profile of v0, /device:TPU:41, one launch (start us, length us, event | category | flops | bytes accessed | tf_op | source)
XLA Modules:
  0.0 316.8 jit_solution(7449039841433495899)
XLA Ops:
  7.2 0.8 broadcast_add_fusion
  8.0 1.0 maximum_maximum_fusion
  9.1 2.9 collective-permute-start.1
  11.9 2.3 collective-permute-start
  14.2 0.7 multiply_subtract_fusion
  15.6 0.7 copy.29
  16.3 16.6 %all-to-all-start = ((s32[128,1,4]{2,1,0:T(1,128)}), s32[128,1,4]{2,1,0:T(1,128)S(1)}, u32[]{:S(2)}, u32[]{:S(2)}) async-start(s32[128,1,4]{2,1,0:T(1,128)} %copy.29), calls=%async_computation | async-start | bytes 131072 | tf_op jit(solution)/shard_map/all_to_all | solution.py:69
  33.0 0.7 all-gather.3.cloned.1.call-update
  33.7 1.2 copy.30
  35.1 1.2 fusion.52
  37.0 0.4 fusion.55
  38.5 0.4 fusion.57
  42.6 0.5 convolution_convert_fusion.1
  43.0 1.2 all_to_all.16
  44.3 13.7 %all-to-all-start.1 = ((bf16[128,4,1024]{2,1,0:T(4,128)(2,1)}), bf16[128,4,1024]{2,1,0:T(4,128)(2,1)S(1)}, u32[]{:S(2)}, u32[]{:S(2)}) async-start(bf16[128,4,1024]{2,1,0:T(4,128)(2,1)} %all_to_all.16), calls=%async_computation.1 | async-start | bytes 2097152 | tf_op jit(solution)/shard_map/all_to_all | solution.py:81
  58.1 1.3 gather_fusion
  59.4 0.5 broadcast.182
  59.9 0.8 reduce.5
  60.8 26.4 %all-to-all-done.1 = bf16[128,4,1024]{2,1,0:T(4,128)(2,1)S(1)} async-done(((bf16[128,4,1024]{2,1,0:T(4,128)(2,1)}), bf16[128,4,1024]{2,1,0:T(4,128)(2,1)S(1)}, u32[]{:S(2)}, u32[]{:S(2)}) %all-to-all-start.1) | async-done | bytes 1048608 | tf_op jit(solution)/shard_map/all_to_all | solution.py:81
  87.2 1.1 all_to_all.18
  88.3 1.7 convolution_convert_fusion.2
  90.0 46.0 %all-gather.3.cloned.1.call-done = bf16[128,12,1024]{2,1,0:T(8,128)(2,1)} async-done(((bf16[1,12,1024]{2,1,0:T(8,128)(2,1)}), bf16[128,12,1024]{2,1,0:T(8,128)(2,1)}) %all-gather.3.cloned.1.call-update) | async-done | bytes 3145744 | tf_op jit(solution)/shard_map/all_gather | solution.py:84
  136.0 6.2 %reshape.159 = bf16[1536,1024]{1,0:T(8,128)(2,1)} reshape(bf16[128,12,1024]{2,1,0:T(8,128)(2,1)} %all-gather.3.cloned.1.call-done) | data formatting | bytes 6291456
  142.2 4.1 %fusion.60 = f32[256,1536]{1,0:T(8,128)} fusion(bf16[256,1024]{1,0:T(8,128)(2,1)S(1)} %convolution_convert_fusion.2, bf16[1536,1024]{1,0:T(8,128)(2,1)} %reshape.159), kind=kOutput, calls=%fused_computation.134 | convolution fusion | flops 805306368 | bytes 5242880 | tf_op jit(solution)/shard_map/tf,nf->tn/dot_general | solution.py:85
  146.2 33.8 %all-reduce.1 = bf16[256,1536]{1,0:T(8,128)(2,1)S(1)} all-reduce(f32[256,1536]{1,0:T(8,128)} %fusion.60), channel_id=1, replica_groups=mesh['seq'=128,'tp'=4] {'tp'}, use_global_device_ids=true, to_apply=%region_18.19 | all-reduce | flops 393216 | bytes 2359296 | tf_op jit(solution)/shard_map/psum | solution.py:86
  180.0 2.7 convolution_convert_fusion
  182.7 6.1 %convert_element_type.112 = bf16[128,12,1024]{2,1,0:T(8,128)(2,1)} reshape(bf16[1536,1024]{1,0:T(8,128)(2,1)} %convolution_convert_fusion) | data formatting | bytes 6291456 | tf_op jit(solution)/shard_map/convert_element_type | solution.py:95
  188.8 13.8 %all-to-all-start.2 = ((bf16[128,12,1024]{2,1,0:T(8,128)(2,1)}), bf16[128,12,1024]{2,1,0:T(8,128)(2,1)}, u32[]{:S(2)}, u32[]{:S(2)}) async-start(bf16[128,12,1024]{2,1,0:T(8,128)(2,1)} %convert_element_type.112), calls=%async_computation.2 | async-start | bytes 8388608 | tf_op jit(solution)/shard_map/all_to_all | solution.py:94
  202.6 0.7 constant_dynamic-slice_fusion
  203.3 103.0 %all-to-all-done.2 = bf16[128,12,1024]{2,1,0:T(8,128)(2,1)} async-done(((bf16[128,12,1024]{2,1,0:T(8,128)(2,1)}), bf16[128,12,1024]{2,1,0:T(8,128)(2,1)}, u32[]{:S(2)}, u32[]{:S(2)}) %all-to-all-start.2) | async-done | bytes 3145760 | tf_op jit(solution)/shard_map/all_to_all | solution.py:94
  306.3 3.0 convert_reduce_fusion
  309.3 0.6 broadcast_multiply_fusion
  (53 shorter events, 6.4 us)
Async XLA Ops:
  7.2 50.9 %copy-start = (bf16[256,1536]{1,0:T(8,128)(2,1)S(1)}, bf16[256,1536]{1,0:T(8,128)(2,1)}, u32[]{:S(2)}) copy-start(bf16[256,1536]{1,0:T(8,128)(2,1)} %param.14) | copy-start | bytes 2359300
  7.2 29.1 %copy-start.1 = (bf16[256,128]{1,0:T(8,128)(2,1)S(1)}, bf16[256,128]{1,0:T(8,128)(2,1)}, u32[]{:S(2)}) copy-start(bf16[256,128]{1,0:T(8,128)(2,1)} %param.9) | copy-start | bytes 196612
  9.1 25.9 %collective-permute-start.1 = (bf16[528,128]{1,0:T(8,128)(2,1)S(1)}, bf16[528,128]{1,0:T(8,128)(2,1)S(1)}, u32[]{:S(2)}, u32[]{:S(2)}) collective-permute-start(bf16[528,128]{1,0:T(8,128)(2,1)S(1)} %maximum_maximum_fusion), channel_id=1, source_target_pairs={{0,4},{4,8},{8,12},{12,16},{16,20},{20,24},{24,28},{28,32},{32,36}... | collective-permute-start | bytes 405512 | tf_op jit(solution)/shard_map/ppermute | solution.py:19
  11.9 23.1 %collective-permute-start = (bf16[528,128]{1,0:T(8,128)(2,1)S(1)}, bf16[528,128]{1,0:T(8,128)(2,1)S(1)}, u32[]{:S(2)}, u32[]{:S(2)}) collective-permute-start(bf16[528,128]{1,0:T(8,128)(2,1)S(1)} %maximum_maximum_fusion), channel_id=1, source_target_pairs={{0,8},{4,12},{8,16},{12,20},{16,24},{20,28},{24,32},{28,36},{32,40... | collective-permute-start | bytes 405512 | tf_op jit(solution)/shard_map/ppermute | solution.py:19
  16.3 28.0 %all-to-all-start = ((s32[128,1,4]{2,1,0:T(1,128)}), s32[128,1,4]{2,1,0:T(1,128)S(1)}, u32[]{:S(2)}, u32[]{:S(2)}) async-start(s32[128,1,4]{2,1,0:T(1,128)} %copy.29), calls=%async_computation | async-start | bytes 131072 | tf_op jit(solution)/shard_map/all_to_all | solution.py:69
  33.0 103.0 %all-gather.3.cloned.1.call-start = ((), (), s32[]{:S(2)}) async-start(), calls=%async_computation.3 | async-start | bytes 4227072 | tf_op jit(solution)/shard_map/all_gather | solution.py:84
  38.9 1.2 copy-start.2
  42.5 15.5 %copy-start.3 = (s32[256]{0:T(256)S(1)}, s32[256]{0:T(256)}, u32[]{:S(2)}) copy-start(s32[256]{0:T(256)} %param.15) | copy-start | bytes 3076
  44.3 42.9 %all-to-all-start.1 = ((bf16[128,4,1024]{2,1,0:T(4,128)(2,1)}), bf16[128,4,1024]{2,1,0:T(4,128)(2,1)S(1)}, u32[]{:S(2)}, u32[]{:S(2)}) async-start(bf16[128,4,1024]{2,1,0:T(4,128)(2,1)} %all_to_all.16), calls=%async_computation.1 | async-start | bytes 2097152 | tf_op jit(solution)/shard_map/all_to_all | solution.py:81
  188.8 117.5 %all-to-all-start.2 = ((bf16[128,12,1024]{2,1,0:T(8,128)(2,1)}), bf16[128,12,1024]{2,1,0:T(8,128)(2,1)}, u32[]{:S(2)}, u32[]{:S(2)}) async-start(bf16[128,12,1024]{2,1,0:T(8,128)(2,1)} %convert_element_type.112), calls=%async_computation.2 | async-start | bytes 8388608 | tf_op jit(solution)/shard_map/all_to_all | solution.py:94
Sparse Core Ops, SparseCore 0:
  36.9 99.0 all-gather.2
where the time goes:
time: 318 us; the launch traced here: 317 us
  waiting for transfers between devices  176 us (55%)
  starting transfers between devices  49.4 us (16%)
  blocking collectives  33.8 us (11%)
  local copies, waits for them, and re-layouts  19.7 us (6%)
  matrix products  14.9 us (5%)
  between operations  14.4 us (5%)
  other arithmetic  8.56 us (3%)
    all_to_all x1, waiting for transfers between devices, on_device(): lax.all_to_all(pieces.astype(jnp.bfloat16), 'seq', split_axis=0, concat_a...  103 us
    all_gather x1, waiting for transfers between devices, on_device(): all_proj = lax.all_gather(proj, 'seq', axis=0, tiled=True)  46 us
    psum x1, blocking collectives, on_device(): y_total = lax.psum(y_part, 'tp')  33.8 us
    all_to_all x1, waiting for transfers between devices, on_device(): lax.all_to_all(buckets, 'seq', split_axis=0, concat_axis=0, tiled=True)  26.4 us
    all_to_all x1, starting transfers between devices, on_device(): lax.all_to_all(slot_table, 'seq', split_axis=0, concat_axis=0, tiled=True)  16.6 us
    all_to_all x1, starting transfers between devices, on_device(): lax.all_to_all(pieces.astype(jnp.bfloat16), 'seq', split_axis=0, concat_a...  13.8 us
    all_to_all x1, starting transfers between devices, on_device(): lax.all_to_all(buckets, 'seq', split_axis=0, concat_axis=0, tiled=True)  13.7 us
    unnamed x10, local copies, waits for them, and re-layouts  7.43 us
  transfers between devices with their start and end apart: 6, of which 3 were waited for; matrix products, arithmetic and copies ran while one was open for 5% of the time, Pallas kernels for 0%

commit v1 on v0

--- a/solution.py
+++ b/solution.py
@@ -11,6 +11,11 @@
 REACH = 2
 GROUP_ROWS = 4
 neg_large = -1e30
+
+
+def gather_and_add(block, mesh_axis):
+    parts = lax.all_gather(block, mesh_axis)
+    return jnp.sum(parts, axis=0)
 
 
 def passed_along(block, axis, distance):
@@ -83,7 +88,7 @@
     student_x = jnp.dot(place, arrived, preferred_element_type=jnp.float32).astype(jnp.bfloat16)
     all_proj = lax.all_gather(proj, "seq", axis=0, tiled=True)
     y_part = jnp.einsum("tf,nf->tn", student_x, all_proj, preferred_element_type=jnp.float32)
-    y_total = lax.psum(y_part, "tp")
+    y_total = gather_and_add(y_part, "tp")
     y_rounded = y_total.astype(jnp.bfloat16)
     delta = (y_rounded.astype(jnp.float32) - targets.astype(jnp.float32)).astype(jnp.bfloat16)
     out_rows = lax.dynamic_slice_in_dim(y_rounded, tp_index * width_share, width_share, 1)

time: 318 us -> 357 us (1.12)
  waiting for transfers between devices: 176 us -> 245 us
  blocking collectives: 33.8 us -> 0 us
    all_gather x0 -> x1, waiting for transfers between devices: none -> 67.3 us  [gather_and_add(): parts = lax.all_gather(block, mesh_axis)]
    psum x1 -> x0, blocking collectives: 33.8 us -> none  [on_device(): y_total = lax.psum(y_part, 'tp')]
  transfers between devices with their start and end apart: 6 -> 7, of which waited for: 3 -> 4; matrix products, arithmetic and copies ran while one was open for 5% -> 5% of each run, Pallas kernels for 0% -> 0%
where the time goes in v1:
time: 357 us; the launch traced here: 356 us
  waiting for transfers between devices  245 us (69%)
  starting transfers between devices  50.8 us (14%)
  local copies, waits for them, and re-layouts  19.7 us (6%)
  matrix products  14.9 us (4%)
  between operations  14.4 us (4%)
  other arithmetic  12.1 us (3%)
    all_to_all x1, waiting for transfers between devices, on_device(): lax.all_to_all(pieces.astype(jnp.bfloat16), 'seq', split_axis=0, concat_a...  103 us
    all_gather x1, waiting for transfers between devices, gather_and_add(): parts = lax.all_gather(block, mesh_axis)  67.3 us
    all_gather x1, waiting for transfers between devices, on_device(): all_proj = lax.all_gather(proj, 'seq', axis=0, tiled=True)  46 us
    all_to_all x1, waiting for transfers between devices, on_device(): lax.all_to_all(buckets, 'seq', split_axis=0, concat_axis=0, tiled=True)  27.5 us
    all_to_all x1, starting transfers between devices, on_device(): lax.all_to_all(slot_table, 'seq', split_axis=0, concat_axis=0, tiled=True)  16.6 us
    all_to_all x1, starting transfers between devices, on_device(): lax.all_to_all(pieces.astype(jnp.bfloat16), 'seq', split_axis=0, concat_a...  15 us
    all_to_all x1, starting transfers between devices, on_device(): lax.all_to_all(buckets, 'seq', split_axis=0, concat_axis=0, tiled=True)  13.7 us
    unnamed x10, local copies, waits for them, and re-layouts  7.43 us
  transfers between devices with their start and end apart: 7, of which 4 were waited for; matrix products, arithmetic and copies ran while one was open for 5% of the time, Pallas kernels for 0%

profile of v1, /device:TPU:41, one launch (start us, length us, event | category | flops | bytes accessed | tf_op | source)
XLA Modules:
  0.0 356.4 jit_solution(12999609048180297622)
XLA Ops:
  7.2 0.8 broadcast_add_fusion
  8.0 1.0 maximum_maximum_fusion
  9.1 2.9 collective-permute-start.1
  11.9 2.3 collective-permute-start
  14.2 0.7 multiply_subtract_fusion
  15.6 0.7 copy.29
  16.3 16.6 %all-to-all-start = ((s32[128,1,4]{2,1,0:T(1,128)}), s32[128,1,4]{2,1,0:T(1,128)S(1)}, u32[]{:S(2)}, u32[]{:S(2)}) async-start(s32[128,1,4]{2,1,0:T(1,128)} %copy.29), calls=%async_computation | async-start | bytes 131072 | tf_op jit(solution)/shard_map/all_to_all | solution.py:74
  33.0 0.7 all-gather.7.cloned.1.call-update
  33.7 1.2 copy.30
  35.1 1.2 fusion.52
  36.6 0.4 fusion.54
  42.6 0.5 convolution_convert_fusion.1
  43.1 1.2 all_to_all.16
  44.3 13.7 %all-to-all-start.1 = ((bf16[128,4,1024]{2,1,0:T(4,128)(2,1)}), bf16[128,4,1024]{2,1,0:T(4,128)(2,1)S(1)}, u32[]{:S(2)}, u32[]{:S(2)}) async-start(bf16[128,4,1024]{2,1,0:T(4,128)(2,1)} %all_to_all.16), calls=%async_computation.1 | async-start | bytes 2097152 | tf_op jit(solution)/shard_map/all_to_all | solution.py:86
  58.3 0.5 broadcast.182
  58.8 0.8 reduce.5
  59.7 27.5 %all-to-all-done.1 = bf16[128,4,1024]{2,1,0:T(4,128)(2,1)S(1)} async-done(((bf16[128,4,1024]{2,1,0:T(4,128)(2,1)}), bf16[128,4,1024]{2,1,0:T(4,128)(2,1)S(1)}, u32[]{:S(2)}, u32[]{:S(2)}) %all-to-all-start.1) | async-done | bytes 1048608 | tf_op jit(solution)/shard_map/all_to_all | solution.py:86
  87.2 1.1 all_to_all.18
  88.3 1.7 convolution_convert_fusion.2
  90.0 46.0 %all-gather.7.cloned.1.call-done = bf16[128,12,1024]{2,1,0:T(8,128)(2,1)} async-done(((bf16[1,12,1024]{2,1,0:T(8,128)(2,1)}), bf16[128,12,1024]{2,1,0:T(8,128)(2,1)}) %all-gather.7.cloned.1.call-update) | async-done | bytes 3145744 | tf_op jit(solution)/shard_map/all_gather | solution.py:89
  136.0 6.2 %reshape.160 = bf16[1536,1024]{1,0:T(8,128)(2,1)} reshape(bf16[128,12,1024]{2,1,0:T(8,128)(2,1)} %all-gather.7.cloned.1.call-done) | data formatting | bytes 6291456
  142.2 4.1 %fusion.60 = f32[256,1536]{1,0:T(8,128)} fusion(bf16[256,1024]{1,0:T(8,128)(2,1)S(1)} %convolution_convert_fusion.2, bf16[1536,1024]{1,0:T(8,128)(2,1)} %reshape.160), kind=kOutput, calls=%fused_computation.134 | convolution fusion | flops 805306368 | bytes 5242880 | tf_op jit(solution)/shard_map/tf,nf->tn/dot_general | solution.py:90
  146.3 1.3 gather_fusion
  147.6 67.3 %all-gather.5.cloned.1.call-done = f32[1024,1536]{1,0:T(8,128)} async-done(((f32[256,1536]{1,0:T(8,128)}), f32[1024,1536]{1,0:T(8,128)}) %all-gather.5.cloned.1.call-update) | async-done | bytes 6291472 | tf_op jit(solution)/shard_map/all_gather | solution.py:17
  214.9 3.5 reduce_sum.111
  218.4 2.7 convolution_convert_fusion
  221.1 6.1 %convert_element_type.112 = bf16[128,12,1024]{2,1,0:T(8,128)(2,1)} reshape(bf16[1536,1024]{1,0:T(8,128)(2,1)} %convolution_convert_fusion) | data formatting | bytes 6291456 | tf_op jit(solution)/shard_map/convert_element_type | solution.py:100
  227.2 15.0 %all-to-all-start.2 = ((bf16[128,12,1024]{2,1,0:T(8,128)(2,1)}), bf16[128,12,1024]{2,1,0:T(8,128)(2,1)}, u32[]{:S(2)}, u32[]{:S(2)}) async-start(bf16[128,12,1024]{2,1,0:T(8,128)(2,1)} %convert_element_type.112), calls=%async_computation.2 | async-start | bytes 8388608 | tf_op jit(solution)/shard_map/all_to_all | solution.py:99
  242.2 0.7 constant_dynamic-slice_fusion
  242.9 103.0 %all-to-all-done.2 = bf16[128,12,1024]{2,1,0:T(8,128)(2,1)} async-done(((bf16[128,12,1024]{2,1,0:T(8,128)(2,1)}), bf16[128,12,1024]{2,1,0:T(8,128)(2,1)}, u32[]{:S(2)}, u32[]{:S(2)}) %all-to-all-start.2) | async-done | bytes 3145760 | tf_op jit(solution)/shard_map/all_to_all | solution.py:99
  345.9 3.0 convert_reduce_fusion
  348.9 0.6 broadcast_multiply_fusion
  (56 shorter events, 7.0 us)
Async XLA Ops:
  7.2 139.1 %copy-start = (bf16[256,1536]{1,0:T(8,128)(2,1)S(1)}, bf16[256,1536]{1,0:T(8,128)(2,1)}, u32[]{:S(2)}) copy-start(bf16[256,1536]{1,0:T(8,128)(2,1)} %param.14) | copy-start | bytes 2359300
  7.2 29.1 %copy-start.1 = (bf16[256,128]{1,0:T(8,128)(2,1)S(1)}, bf16[256,128]{1,0:T(8,128)(2,1)}, u32[]{:S(2)}) copy-start(bf16[256,128]{1,0:T(8,128)(2,1)} %param.9) | copy-start | bytes 196612
  9.1 25.9 %collective-permute-start.1 = (bf16[528,128]{1,0:T(8,128)(2,1)S(1)}, bf16[528,128]{1,0:T(8,128)(2,1)S(1)}, u32[]{:S(2)}, u32[]{:S(2)}) collective-permute-start(bf16[528,128]{1,0:T(8,128)(2,1)S(1)} %maximum_maximum_fusion), channel_id=1, source_target_pairs={{0,4},{4,8},{8,12},{12,16},{16,20},{20,24},{24,28},{28,32},{32,36}... | collective-permute-start | bytes 405512 | tf_op jit(solution)/shard_map/ppermute | solution.py:24
  11.9 23.1 %collective-permute-start = (bf16[528,128]{1,0:T(8,128)(2,1)S(1)}, bf16[528,128]{1,0:T(8,128)(2,1)S(1)}, u32[]{:S(2)}, u32[]{:S(2)}) collective-permute-start(bf16[528,128]{1,0:T(8,128)(2,1)S(1)} %maximum_maximum_fusion), channel_id=1, source_target_pairs={{0,8},{4,12},{8,16},{12,20},{16,24},{20,28},{24,32},{28,36},{32,40... | collective-permute-start | bytes 405512 | tf_op jit(solution)/shard_map/ppermute | solution.py:24
  16.3 28.0 %all-to-all-start = ((s32[128,1,4]{2,1,0:T(1,128)}), s32[128,1,4]{2,1,0:T(1,128)S(1)}, u32[]{:S(2)}, u32[]{:S(2)}) async-start(s32[128,1,4]{2,1,0:T(1,128)} %copy.29), calls=%async_computation | async-start | bytes 131072 | tf_op jit(solution)/shard_map/all_to_all | solution.py:74
  33.0 103.0 %all-gather.7.cloned.1.call-start = ((), (), s32[]{:S(2)}) async-start(), calls=%async_computation.4 | async-start | bytes 4227072 | tf_op jit(solution)/shard_map/all_gather | solution.py:89
  38.9 1.2 copy-start.2
  44.3 42.9 %all-to-all-start.1 = ((bf16[128,4,1024]{2,1,0:T(4,128)(2,1)}), bf16[128,4,1024]{2,1,0:T(4,128)(2,1)S(1)}, u32[]{:S(2)}, u32[]{:S(2)}) async-start(bf16[128,4,1024]{2,1,0:T(4,128)(2,1)} %all_to_all.16), calls=%async_computation.1 | async-start | bytes 2097152 | tf_op jit(solution)/shard_map/all_to_all | solution.py:86
  58.0 156.8 %all-gather.5.cloned.1.call-start = ((), (), s32[]{:S(2)}) async-start(), calls=%async_computation.3 | async-start | bytes 7864320 | tf_op jit(solution)/shard_map/all_gather | solution.py:17
  142.2 4.1 %copy-start.3 = (s32[256]{0:T(256)S(1)}, s32[256]{0:T(256)}, u32[]{:S(2)}) copy-start(s32[256]{0:T(256)} %param.15) | copy-start | bytes 3076
  227.2 118.7 %all-to-all-start.2 = ((bf16[128,12,1024]{2,1,0:T(8,128)(2,1)}), bf16[128,12,1024]{2,1,0:T(8,128)(2,1)}, u32[]{:S(2)}, u32[]{:S(2)}) async-start(bf16[128,12,1024]{2,1,0:T(8,128)(2,1)} %convert_element_type.112), calls=%async_computation.2 | async-start | bytes 8388608 | tf_op jit(solution)/shard_map/all_to_all | solution.py:99
Sparse Core Ops, SparseCore 0:
  36.9 99.0 all-gather.6
  146.4 68.4 all-gather.4
